TPU v7x, 128 devices: a whole 4x4x4 slice. The times are simulated.
128 devices in a mesh: blk: 16 (over y_hi, x, core), occ: 8 (over z, y_lo).
Axes of the slice: x: 4, y: 4 (y_hi: 2, y_lo: 2; y = y_hi * 2 + y_lo), z: 4, core: 2. Of those that a mesh axis runs over, the one named last changes fastest.
Arguments:
- amplitudes: bfloat16 [8, 512, 163840], P(None, 'blk', 'occ'), may hold values from -6 to 6
- cholesky: bfloat16 [4096, 4096], P('occ'), may hold values from -0.09375 to 0.09375
- virtual_order: int32 [64], replicated, may hold values from 0 to 63, each once
Outputs:
- residual: bfloat16 [8, 512, 163840], P(None, 'blk', 'occ')
Inputs may be any that keep to these rules, and one draw needn't show every extreme that they name: The orbitals of irrep h are virtual_order[h * 8 + u] for u < 8; every orbital appears once.
All inputs are finite; a program needn't handle non-finite values.
Results may differ from a plain program's by a relative error of at most 0.0051.
Values may be sent and summed in bfloat16 or wider, within the bound.
A program may use at most 192 MiB of HBM per device.

v0:
```python
import jax
import jax.numpy as jnp
import numpy as np
from jax import lax
from jax.sharding import PartitionSpec as P


def body(amplitudes, cholesky, virtual_order):
    blk_count = lax.axis_size("blk")
    me_blk = lax.axis_index("blk")
    vir_count = virtual_order.shape[0]
    per_irrep = vir_count // 8
    tile_size = vir_count // blk_count
    slot_count = vir_count * per_irrep
    regrouped = lax.all_to_all(amplitudes, "blk", split_axis=2, concat_axis=1, tiled=True)
    vectors = cholesky.reshape(cholesky.shape[0], vir_count, vir_count)
    sorted_vec = jnp.take(jnp.take(vectors, virtual_order, axis=1), virtual_order, axis=2)
    tile_start = me_blk * tile_size
    tile_rows = lax.dynamic_slice_in_dim(sorted_vec, tile_start, tile_size, 1)
    tile_rows = tile_rows.reshape(cholesky.shape[0], tile_size, 8, per_irrep)
    tile_irrep = tile_start // per_irrep
    partial_rows = []
    for symmetry in range(8):
        partner = jnp.bitwise_xor(tile_irrep, symmetry)
        irrep_block = lax.dynamic_slice_in_dim(sorted_vec, partner * per_irrep, per_irrep, 1)
        irrep_block = irrep_block.reshape(cholesky.shape[0], per_irrep, 8, per_irrep)
        irrep_block = irrep_block[:, :, np.arange(8) ^ symmetry, :]
        product_rows = jnp.einsum(
            "qakx,qwky->awkxy", tile_rows, irrep_block, preferred_element_type=jnp.float32
        )
        partial_rows.append(product_rows.reshape(tile_size * per_irrep, slot_count))
    partial_value = jnp.stack(partial_rows)
    summed_rows = lax.psum(partial_value, "occ").astype(jnp.bfloat16)
    ladder = jnp.einsum(
        "grs,gsp->grp",
        lax.all_gather(summed_rows, "blk", axis=1, tiled=True),
        regrouped,
        preferred_element_type=jnp.float32,
    )
    ladder = ladder.astype(jnp.bfloat16)
    return lax.all_to_all(ladder, "blk", split_axis=1, concat_axis=2, tiled=True)


def solution(mesh):
    placed = (P(None, "blk", "occ"), P("occ", None), P())
    return jax.shard_map(
        body, mesh=mesh, in_specs=placed, out_specs=P(None, "blk", "occ"), check_vma=False
    )
```

profile of v0, /device:TPU:1, one launch (start us, length us, event | category | flops | bytes accessed | tf_op | source)
XLA Modules:
  0.0 515.6 jit_solution(4875041902164769643)
XLA Ops:
  6.5 39.9 %copy.112 = bf16[8,32,20480]{1,0,2:T(8,128)(2,1)} copy(bf16[8,32,20480]{2,1,0:T(8,128)(2,1)} %param.19) | data formatting | bytes 20971520 | tf_op args[0]
  46.5 43.6 %reshape.143 = bf16[16,2,163840]{2,1,0:T(2,128)(2,1)} reshape(bf16[20480,8,32]{2,1,0:T(8,128)(2,1)} %bitcast.126) | data formatting | bytes 20971520
  90.1 8.6 %all-to-all-start = ((bf16[16,2,163840]{2,1,0:T(2,128)(2,1)}), bf16[16,2,163840]{2,1,0:T(2,128)(2,1)}, u32[]{:S(2)}, u32[]{:S(2)}) async-start(bf16[16,2,163840]{2,1,0:T(2,128)(2,1)} %reshape.143), calls=%async_computation | async-start | bytes 20971520 | tf_op jit(solution)/shard_map/all_to_all | solution.py:15
  98.6 0.0 all-gather.2.cloned.1.call-start
  98.7 0.0 copy-done.10
  98.8 6.6 %copy.69 = bf16[512,4096]{0,1:T(8,128)(2,1)} copy(bf16[512,4096]{1,0:T(8,128)(2,1)} %param.20) | data formatting | bytes 8388608 | tf_op args[1]
  105.4 5.0 gather_fusion
  110.4 2.6 select_bitcast_fusion
  113.0 4.3 copy.70
  117.3 5.0 gather_fusion.1
  122.3 4.6 broadcast_select_fusion
  126.9 0.0 copy-done.9
  127.0 1.2 dynamic-slice_bitcast_fusion
  128.2 3.6 constant_dynamic-slice_fusion
  131.8 1.6 gather_fusion.2
  133.4 1.9 convolution_bitcast_fusion.7
  135.3 2.6 copy.76
  137.8 1.7 stack_reshape.24
  139.6 0.0 copy-start.8
  139.6 1.6 gather_fusion.3
  141.2 1.9 convolution_bitcast_fusion.6
  143.1 2.6 copy.81
  145.7 1.7 stack_reshape.25
  147.4 0.0 copy-done.7
  147.4 0.0 copy-done.8
  147.4 1.6 gather_fusion.4
  149.1 1.9 convolution_bitcast_fusion.5
  150.9 2.5 copy.86
  153.5 2.4 stack_reshape.26
  155.9 0.6 gather_fusion.5
  156.4 1.9 convolution_bitcast_fusion.4
  158.3 1.6 copy.91
  159.9 1.1 stack_reshape.27
  161.0 0.0 copy-done.5
  161.0 0.0 copy-done.6
  161.0 0.6 gather_fusion.6
  161.6 1.9 convolution_bitcast_fusion.3
  163.5 1.6 copy.96
  165.0 1.1 stack_reshape.28
  166.2 0.6 gather_fusion.7
  166.8 0.9 convolution_bitcast_fusion.2
  167.7 0.3 copy.101
  168.0 0.7 stack_reshape.29
  168.7 0.0 copy-done.3
  168.7 0.0 copy-done.4
  168.8 0.6 gather_fusion.8
  169.3 0.9 convolution_bitcast_fusion.1
  170.2 0.3 copy.106
  170.6 0.5 stack_reshape.30
  171.1 0.6 gather_fusion.9
  171.7 0.9 convolution_bitcast_fusion
  172.6 0.3 copy.111
  172.9 0.5 stack_reshape.31
  173.6 72.4 %all-reduce.1 = bf16[8,32,512]{2,1,0:T(8,128)(2,1)} all-reduce(f32[8,32,512]{2,1,0:T(8,128)S(1)} %constant_dynamic-update-slice_fusion), channel_id=1, replica_groups=mesh['blk'=16,'occ'=8] {'occ'}, use_global_device_ids=true, to_apply=%region_0.1 | all-reduce | flops 131072 | bytes 786432 | tf_op jit(solution)/shard_map/psum | solution.py:33
  245.9 0.0 all-gather.2.cloned.1.call-update
  245.9 0.0 all-to-all-done
  246.0 26.2 %reshape.144 = bf16[20480,8,32]{2,1,0:T(8,128)(2,1)} reshape(bf16[16,2,163840]{2,1,0:T(2,128)(2,1)} %all-to-all-done) | data formatting | bytes 20971520
  272.1 42.1 %copy.113 = bf16[8,32,16,1280]{3,1,2,0:T(8,128)(2,1)} copy(bf16[8,32,16,1280]{1,0,3,2:T(8,128)(2,1)} %bitcast.125) | data formatting | bytes 20971520 | tf_op jit(solution)/shard_map/all_to_all | solution.py:15
  314.2 1.0 all-gather.2.cloned.1.call-done
  315.2 12.8 %convolution_convert_fusion = bf16[8,512,1280]{2,1,0:T(8,128)(2,1)} fusion(bf16[8,512,512]{2,1,0:T(8,128)(2,1)} %all-gather.2.cloned.1.call-done, bf16[8,512,1280]{2,1,0:T(8,128)(2,1)} %bitcast.145), kind=kOutput, calls=%fused_computation.10 | convolution fusion | flops 5373952000 | bytes 25165824 | tf_op jit(solution)/shard_map/grs,gsp->grp/dot_general | solution.py:34
  328.0 13.9 %copy.114 = bf16[8,512,1280]{2,0,1:T(8,128)(2,1)} copy(bf16[8,512,1280]{2,1,0:T(8,128)(2,1)} %convolution_convert_fusion) | data formatting | bytes 20971520 | tf_op jit(solution)/shard_map/convert_element_type | solution.py:40
  341.9 138.0 %all_to_all.36 = bf16[8,512,1280]{2,0,1:T(8,128)(2,1)} all-to-all(bf16[8,512,1280]{2,0,1:T(8,128)(2,1)} %copy.114), channel_id=1, replica_groups=mesh['blk'=16,'occ'=8] {'blk'}, dimensions={1} | all-to-all | bytes 20971520 | tf_op jit(solution)/shard_map/all_to_all | solution.py:41
  479.9 13.7 %copy.115 = bf16[8,32,16,1280]{3,2,1,0:T(8,128)(2,1)} copy(bf16[8,32,16,1280]{3,0,1,2:T(8,128)(2,1)} %bitcast.143) | data formatting | bytes 20971520 | tf_op jit(solution)/shard_map/all_to_all | solution.py:41
  493.6 14.8 %all_to_all.33 = bf16[8,32,20480]{2,1,0:T(8,128)(2,1)} reshape(bf16[8,32,16,1280]{3,2,1,0:T(8,128)(2,1)} %copy.115) | data formatting | bytes 20971520 | tf_op jit(solution)/shard_map/all_to_all | solution.py:41
  (29 shorter events, 0.1 us)
Async XLA Ops:
  90.1 8.7 %copy-start.10 = (s32[64]{0:T(128)S(1)}, s32[64]{0:T(128)}, u32[]{:S(2)}) copy-start(s32[64]{0:T(128)} %param.21) | copy-start | bytes 772
  90.1 155.9 %all-to-all-start = ((bf16[16,2,163840]{2,1,0:T(2,128)(2,1)}), bf16[16,2,163840]{2,1,0:T(2,128)(2,1)}, u32[]{:S(2)}, u32[]{:S(2)}) async-start(bf16[16,2,163840]{2,1,0:T(2,128)(2,1)} %reshape.143), calls=%async_computation | async-start | bytes 20971520 | tf_op jit(solution)/shard_map/all_to_all | solution.py:15
  98.6 216.6 %all-gather.2.cloned.1.call-start = ((), (), s32[]{:S(2)}) async-start(), calls=%async_computation.2 | async-start | bytes 4456448 | tf_op jit(solution)/shard_map/all_gather | solution.py:36
  122.3 4.6 copy-start.9
  139.6 7.8 %copy-start.7 = (s32[8]{0:T(128)S(1)}, s32[8]{0:T(128)}, u32[]{:S(2)}) copy-start(s32[8]{0:T(128)} %constant.99) | copy-start | bytes 100
  139.6 7.8 %copy-start.8 = (s32[8]{0:T(128)S(1)}, s32[8]{0:T(128)}, u32[]{:S(2)}) copy-start(s32[8]{0:T(128)} %constant.98) | copy-start | bytes 100
  155.9 5.2 copy-start.5
  155.9 5.2 %copy-start.6 = (s32[8]{0:T(128)S(1)}, s32[8]{0:T(128)}, u32[]{:S(2)}) copy-start(s32[8]{0:T(128)} %constant.100) | copy-start | bytes 100
  166.2 2.5 copy-start.3
  166.2 2.5 copy-start.4
  171.1 2.4 copy-start
  171.1 2.4 copy-start.1
  171.1 2.4 copy-start.2
Sparse Core Ops, SparseCore 0:
  246.1 69.0 all-gather.1
where the time goes:
time: 525 us; the launch traced here: 516 us
  local copies, waits for them, and re-layouts  249 us (47%)
  blocking collectives  210 us (40%)
  matrix products  24.7 us (5%)
  between operations  14.2 us (3%)
  starting transfers between devices  8.6 us (2%)
  other arithmetic  7.29 us (1%)
    all_to_all x1, blocking collectives, body(): lax.all_to_all(ladder, 'blk', split_axis=1, concat_axis=2, tiled=True)  138 us
    unnamed x34, local copies, waits for them, and re-layouts  120 us
    psum x1, blocking collectives, body(): summed_rows = lax.psum(partial_value, 'occ').astype(jnp.bfloat16)  72.4 us
    all_to_all x1, local copies, waits for them, and re-layouts, body(): lax.all_to_all(amplitudes, 'blk', split_axis=2, concat_axis=1, tiled=True)  42.1 us
    all_to_all x2, local copies, waits for them, and re-layouts, body(): lax.all_to_all(ladder, 'blk', split_axis=1, concat_axis=2, tiled=True)  28.4 us
    convert_element_type x1, local copies, waits for them, and re-layouts, body(): ladder = ladder.astype(jnp.bfloat16)  13.9 us
    dot_general x1, matrix products, body(): jnp.einsum('grs,gsp->grp', lax.all_gather(summed_rows, 'blk', axis=1, til...  12.8 us
    dot_general x8, matrix products, body(): jnp.einsum('qakx,qwky->awkxy', tile_rows, irrep_block, preferred_element_...  12 us
  transfers between devices with their start and end apart: 2, of which 1 were waited for; matrix products, arithmetic and copies ran while one was open for 28% of the time, Pallas kernels for 0%

commit v1 on v0

v1 whole, which is shorter than its diff:
```python
import functools

import jax
import jax.numpy as jnp
from jax import lax
from jax.experimental import pallas as pl
from jax.experimental.pallas import tpu as pltpu
from jax.sharding import PartitionSpec as P

MESH = pl.DeviceIdType.MESH
CHUNKS = 8
FIRST, SECOND = 4, 6
HOPS = ((0, 1), (0, 3), (1, 0), (0, 2), (1, 1), (1, 3), (1, 2), (0, 0))
PEERS = tuple((dy, dx, dc) for dc in (0, 1) for dy, dx in HOPS if (dy, dx, dc) != (0, 0, 0))
NT = (((1,), (1,)), ((), ()))


def xor8(a, b):
    return sum(2**i * ((a // 2**i % 2 + b // 2**i % 2) % 2) for i in range(3))


def dot(a, b, dims=(((1,), (0,)), ((), ()))):
    return lax.dot_general(a, b, dims, preferred_element_type=jnp.float32)


def iota(shape, axis):
    return lax.broadcasted_iota(jnp.int32, shape, axis)


def kernel(
    order, amp, chol, res,
    slots, out, vec, srt, brow, arow, gram, part, gath, mine, full, ints,
    in_s, in_r, back_s, back_r, red_s, red_r, all_s, all_r, own_in, own_out, vec_sem,
):
    blk, occ = lax.axis_index("blk"), lax.axis_index("occ")
    y_hi, x_at, core = blk // 8, blk // 2 % 4, blk % 2
    sym = blk // 2
    width = slots.shape[1]
    step = width // CHUNKS
    rows = slots.shape[0] // 16

    def peer(offset):
        dy, dx, dc = offset
        return (y_hi + dy) % 2 * 8 + (x_at + dx) % 4 * 2 + (core + dc) % 2

    def occ_peer(d, e):
        return {"blk": sym * 2 + (core + e) % 2, "occ": (occ + d) % 8}

    others = [(d, e) for e in (0, 1) for d in range(8) if (d, e) != (0, 0)]

    load = pltpu.make_async_copy(chol, vec, vec_sem)
    load.start()
    keep = pltpu.make_async_copy(
        amp.at[sym, :, pl.ds(pl.multiple_of(core * width, 128), width)],
        slots.at[pl.ds(pl.multiple_of(blk * rows, 32), rows), :],
        own_in,
    )
    keep.start()

    barrier = pltpu.get_barrier_semaphore()
    for offset in PEERS:
        pl.semaphore_signal(barrier, inc=1, device_id={"blk": peer(offset)}, device_id_type=MESH)
    for d, e in others:
        if d:
            pl.semaphore_signal(barrier, inc=1, device_id=occ_peer(d, e), device_id_type=MESH)
    pl.semaphore_wait(barrier, len(PEERS) + 14)

    def columns(half, s):
        return pl.ds(pl.multiple_of(half * width + s * step, 128), step)

    def block(at):
        return pl.ds(pl.multiple_of(at * rows, 32), rows)

    def send_in(i, s):
        to = peer(PEERS[i])
        return pltpu.make_async_remote_copy(
            src_ref=amp.at[to // 2, :, columns(to % 2, s)],
            dst_ref=slots.at[block(blk), columns(0, s)],
            send_sem=in_s.at[i, s],
            recv_sem=in_r.at[i, s],
            device_id={"blk": to},
            device_id_type=MESH,
        )

    def send_back(i, s):
        to = peer(PEERS[i])
        return pltpu.make_async_remote_copy(
            src_ref=out.at[block(to), columns(0, s)],
            dst_ref=res.at[sym, :, columns(core, s)],
            send_sem=back_s.at[i, s],
            recv_sem=back_r.at[i, s],
            device_id={"blk": to},
            device_id_type=MESH,
        )

    def keep_back(s):
        return pltpu.make_async_copy(
            out.at[block(blk), columns(0, s)], res.at[sym, :, columns(core, s)], own_out.at[s]
        )

    def start_in(first, last):
        @pl.loop(first, last)
        def _(s):
            for i in range(len(PEERS)):
                send_in(i, s).start()

    start_in(0, FIRST)

    target = iota((256, 1), 0)
    picked = jnp.zeros((256, 1), jnp.int32)
    for m in range(64):
        picked = jnp.where(target % 64 == m, order[m], picked)
    choose = iota((256, 256), 1) == picked + target // 64 * 64
    choose = choose.astype(jnp.float32).astype(jnp.bfloat16)
    load.wait()

    @pl.loop(0, 16)
    def _(j):
        at = pl.ds(pl.multiple_of(j * 256, 256), 256)
        sorted_vec = dot(choose, vec[:, at], NT).astype(jnp.bfloat16)
        for a in range(4):
            srt[j * 4 + a] = sorted_vec[a * 64 : a * 64 + 64]

    def orbital(irrep, u):
        return srt[order[irrep * 8 + u]]

    lane = iota((8, 1024), 1)
    for local in range(2):
        pair = core * 2 + local

        @pl.loop(0, 8)
        def _(w):
            for h in range(2):
                at = pl.ds(pl.multiple_of(w * 128 + h * 64, 64), 64)
                brow[at, :] = orbital(xor8(pair * 2 + h, sym), w)

        @pl.loop(0, 8)
        def _(u):
            for h in range(2):
                arow[h * 64 : h * 64 + 64, :] = orbital(pair * 2 + h, u)
            product = dot(arow[...], brow[...], NT)
            wanted = lane // 8 % 16
            total = jnp.zeros((8, 1024), jnp.float32)
            for h in range(2):
                for k in range(8):
                    at = h * 64 + k * 8
                    total = jnp.where(wanted == h * 8 + xor8(k, sym), product[at : at + 8], total)
            for w in range(8):
                gram[w, pl.ds(pl.multiple_of(u * 8, 8), 8), :] = total[:, w * 128 : w * 128 + 128]

        for x in range(8):
            for w in range(8):
                part[local * 64 + w * 8 : local * 64 + w * 8 + 8, x * 128 : x * 128 + 128] = gram[
                    w, pl.ds(x, 8, stride=8), :
                ]

    def slice_of(at):
        return pl.ds(pl.multiple_of(at * 16, 16), 16)

    def reduce_to(d):
        return pltpu.make_async_remote_copy(
            src_ref=part.at[slice_of((occ + d) % 8), :],
            dst_ref=gath.at[d - 1],
            send_sem=red_s.at[d],
            recv_sem=red_r.at[d],
            device_id=occ_peer(d, 0),
            device_id_type=MESH,
        )

    for d in range(1, 8):
        reduce_to(d).start()
    start_in(FIRST, SECOND)
    total = part[slice_of(occ), :]
    for d in range(1, 8):
        reduce_to(d).wait_recv()
        total = total + gath[d - 1]
    mine[...] = total.astype(jnp.bfloat16)
    place = pl.ds(pl.multiple_of(core * 128 + occ * 16, 16), 16)
    full[place, :] = total.astype(jnp.bfloat16)

    def share(n):
        d, e = others[n]
        return pltpu.make_async_remote_copy(
            src_ref=mine,
            dst_ref=full.at[place, :],
            send_sem=all_s.at[n],
            recv_sem=all_r.at[n],
            device_id=occ_peer(d, e),
            device_id_type=MESH,
        )

    for n in range(len(others)):
        share(n).start()
    start_in(SECOND, CHUNKS)
    for n in range(len(others)):
        share(n).wait_recv()

    goal, source = iota((1024, 512), 1), iota((1024, 512), 0)
    gk = goal // 64
    other = sum(2**i * ((gk // 2**i % 2 + sym // 2**i % 2) % 2) for i in range(3))
    base = goal // 8 % 8 * 128 + other * 8 + goal % 8
    r, c = iota((256, 256), 0), iota((256, 256), 1)
    swap = c == r // 64 * 64 + r % 8 * 8 + r // 8 % 8
    swap = swap.astype(jnp.float32).astype(jnp.bfloat16)
    for h in range(2):
        pick = (source == base + h * 64).astype(jnp.float32).astype(jnp.bfloat16)
        moved = dot(full[...], pick).astype(jnp.bfloat16)
        moved = dot(swap, moved).astype(jnp.bfloat16)
        for pair in range(4):
            at = (pair * 2 + h) * 64
            ints[at : at + 64, :] = moved[pair * 64 : pair * 64 + 64]

    keep.wait()

    @pl.loop(0, CHUNKS)
    def _(s):
        for i in range(len(PEERS)):
            send_in(i, s).wait_recv()

        @pl.loop(0, step // 256)
        def _(j):
            at = pl.ds(pl.multiple_of(s * step + j * 256, 256), 256)
            out[:, at] = dot(ints[...], slots[:, at]).astype(jnp.bfloat16)

        for i in range(len(PEERS)):
            send_back(i, s).start()
        keep_back(s).start()

    for d in range(1, 8):
        reduce_to(d).wait_send()
    for n in range(len(others)):
        share(n).wait_send()

    @pl.loop(0, CHUNKS)
    def _(s):
        for i in range(len(PEERS)):
            send_in(i, s).wait_send()
        for i in range(len(PEERS)):
            send_back(i, s).wait()
        keep_back(s).wait()


def body(amplitudes, cholesky, virtual_order):
    groups, rows, columns = amplitudes.shape
    width = columns // 2
    sems = pltpu.SemaphoreType.DMA
    peers = len(PEERS)
    vectors = cholesky.shape[0]
    return pl.pallas_call(
        kernel,
        out_shape=jax.ShapeDtypeStruct(amplitudes.shape, jnp.bfloat16),
        in_specs=[
            pl.BlockSpec(memory_space=pltpu.SMEM),
            pl.BlockSpec(memory_space=pl.ANY),
            pl.BlockSpec(memory_space=pl.ANY),
        ],
        out_specs=pl.BlockSpec(memory_space=pl.ANY),
        scratch_shapes=[
            pltpu.VMEM((16 * rows, width), jnp.bfloat16),
            pltpu.VMEM((16 * rows, width), jnp.bfloat16),
            pltpu.VMEM(cholesky.shape, jnp.bfloat16),
            pltpu.VMEM((64, 64, vectors), jnp.bfloat16),
            pltpu.VMEM((1024, vectors), jnp.bfloat16),
            pltpu.VMEM((128, vectors), jnp.bfloat16),
            pltpu.VMEM((8, 64, 128), jnp.float32),
            pltpu.VMEM((128, 1024), jnp.float32),
            pltpu.VMEM((7, 16, 1024), jnp.float32),
            pltpu.VMEM((16, 1024), jnp.bfloat16),
            pltpu.VMEM((256, 1024), jnp.bfloat16),
            pltpu.VMEM((512, 512), jnp.bfloat16),
            sems((peers, CHUNKS)),
            sems((peers, CHUNKS)),
            sems((peers, CHUNKS)),
            sems((peers, CHUNKS)),
            sems((8,)),
            sems((8,)),
            sems((15,)),
            sems((15,)),
            sems,
            sems((CHUNKS,)),
            sems,
        ],
        compiler_params=pltpu.CompilerParams(
            collective_id=0, has_side_effects=True, vmem_limit_bytes=64000 * 1024
        ),
        name="ladder",
    )(virtual_order, amplitudes, cholesky)


def solution(mesh):
    placed = (P(None, "blk", "occ"), P("occ", None), P())
    return jax.shard_map(
        body, mesh=mesh, in_specs=placed, out_specs=P(None, "blk", "occ"), check_vma=False
    )
```

time: 525 us -> 266 us (0.51); the launches traced: 516 us -> 263 us
  Pallas kernels: 0 us -> 254 us
  local copies, waits for them, and re-layouts: 249 us -> 9.16 us
  blocking collectives: 210 us -> 0 us
  matrix products: 24.7 us -> 0 us
  between operations: 14.2 us -> 0.01 us
  starting transfers between devices: 8.6 us -> 0 us
  other arithmetic: 7.29 us -> 0 us
    pallas_call x0 -> x1, Pallas kernels: none -> 254 us  [body(): pl.pallas_call(kernel, out_shape=jax.ShapeDtypeStruct(amplitudes.shape, j...]
    all_to_all x1 -> x0, blocking collectives: 138 us -> none  [body(): lax.all_to_all(ladder, 'blk', split_axis=1, concat_axis=2, tiled=True)]
    unnamed x34 -> x1, local copies, waits for them, and re-layouts: 120 us -> 9.16 us
    psum x1 -> x0, blocking collectives: 72.4 us -> none  [body(): summed_rows = lax.psum(partial_value, 'occ').astype(jnp.bfloat16)]
    all_to_all x3 -> x0, local copies, waits for them, and re-layouts: 70.5 us -> none  [the longest x1 42.1 us: body(): lax.all_to_all(amplitudes, 'blk', split_axis=2, concat_axis=1, tiled=True)]
    dot_general x9 -> x0, matrix products: 24.7 us -> none  [the longest x1 12.8 us: body(): jnp.einsum('grs,gsp->grp', lax.all_gather(summed_rows, 'blk', axis=1, til...]
    gather x10 -> x0, local copies, waits for them, and re-layouts: 17.7 us -> none  [the longest x8 7.77 us: body(): irrep_block = irrep_block[:, :, np.arange(8) ^ symmetry, :]]
    convert_element_type x1 -> x0, local copies, waits for them, and re-layouts: 13.9 us -> none  [body(): ladder = ladder.astype(jnp.bfloat16)]
  transfers between devices with their start and end apart: 2 -> 0, of which waited for: 1 -> 0; matrix products, arithmetic and copies ran while one was open for 28% -> 0% of each run, Pallas kernels for 0% -> 0%
where the time goes in v1:
time: 266 us; the launch traced here: 263 us
  Pallas kernels  254 us (95%)
  local copies, waits for them, and re-layouts  9.16 us (3%)
    pallas_call x1, Pallas kernels, body(): pl.pallas_call(kernel, out_shape=jax.ShapeDtypeStruct(amplitudes.shape, j...  254 us
    unnamed x1, local copies, waits for them, and re-layouts  9.16 us

profile of v1, /device:TPU:1, one launch (start us, length us, event | category | flops | bytes accessed | tf_op | source)
XLA Modules:
  0.0 262.9 jit_solution(3994036650914887029)
XLA Ops:
  0.0 253.8 %ladder.1 = bf16[8,32,20480]{2,1,0:T(8,128)(2,1)} custom-call(s32[64]{0:T(128)} %order.1, bf16[8,32,20480]{2,1,0:T(8,128)(2,1)} %amp.1, bf16[512,4096]{1,0:T(8,128)(2,1)} %chol.1), custom_call_target="tpu_custom_call" | custom-call | tf_op jit(solution)/shard_map/ladder/pallas_call | solution.py:249
  253.8 9.2 %copy.5 = bf16[8,32,20480]{2,1,0:T(8,128)(2,1)} copy(bf16[8,32,20480]{2,1,0:T(8,128)(2,1)} %ladder.1) | data formatting | bytes 20971520

commit v2 on v1

--- a/solution.py
+++ b/solution.py
@@ -28,13 +28,13 @@
 
 
 def kernel(
-    order, amp, chol, res,
-    slots, out, vec, srt, brow, arow, gram, part, gath, mine, full, ints,
-    in_s, in_r, back_s, back_r, red_s, red_r, all_s, all_r, own_in, own_out, vec_sem,
+    orbitals, amp, chol, res,
+    order, slots, out, vec, srt, brow, arow, gram, part, gath, mine, full, ints,
+    in_s, in_r, back_s, back_r, red_s, red_r, all_s, all_r, own_in, own_out, vec_sem, order_sem,
 ):
     blk, occ = lax.axis_index("blk"), lax.axis_index("occ")
     y_hi, x_at, core = blk // 8, blk // 2 % 4, blk % 2
-    sym = blk // 2
+    sym, z_at = blk // 2, occ // 2
     width = slots.shape[1]
     step = width // CHUNKS
     rows = slots.shape[0] // 16
@@ -43,13 +43,15 @@
         dy, dx, dc = offset
         return (y_hi + dy) % 2 * 8 + (x_at + dx) % 4 * 2 + (core + dc) % 2
 
-    def occ_peer(d, e):
-        return {"blk": sym * 2 + (core + e) % 2, "occ": (occ + d) % 8}
-
-    others = [(d, e) for e in (0, 1) for d in range(8) if (d, e) != (0, 0)]
+    def near(d, f, e):
+        return {"blk": sym * 2 + (core + e) % 2, "occ": (z_at + d) % 4 * 2 + (occ + f) % 2}
+
+    others = [(d, e) for e in (0, 1) for d in range(4) if (d, e) != (0, 0)]
 
     load = pltpu.make_async_copy(chol, vec, vec_sem)
     load.start()
+    read = pltpu.make_async_copy(orbitals, order, order_sem)
+    read.start()
     keep = pltpu.make_async_copy(
         amp.at[sym, :, pl.ds(pl.multiple_of(core * width, 128), width)],
         slots.at[pl.ds(pl.multiple_of(blk * rows, 32), rows), :],
@@ -60,10 +62,10 @@
     barrier = pltpu.get_barrier_semaphore()
     for offset in PEERS:
         pl.semaphore_signal(barrier, inc=1, device_id={"blk": peer(offset)}, device_id_type=MESH)
-    for d, e in others:
-        if d:
-            pl.semaphore_signal(barrier, inc=1, device_id=occ_peer(d, e), device_id_type=MESH)
-    pl.semaphore_wait(barrier, len(PEERS) + 14)
+    around = [(d, 0, e) for d, e in others if d] + [(0, 1, 0)]
+    for at in around:
+        pl.semaphore_signal(barrier, inc=1, device_id=near(*at), device_id_type=MESH)
+    pl.semaphore_wait(barrier, len(PEERS) + len(around))
 
     def columns(half, s):
         return pl.ds(pl.multiple_of(half * width + s * step, 128), step)
@@ -106,6 +108,7 @@
 
     start_in(0, FIRST)
 
+    read.wait()
     target = iota((256, 1), 0)
     picked = jnp.zeros((256, 1), jnp.int32)
     for m in range(64):
@@ -154,38 +157,48 @@
                     w, pl.ds(x, 8, stride=8), :
                 ]
 
-    def slice_of(at):
-        return pl.ds(pl.multiple_of(at * 16, 16), 16)
-
-    def reduce_to(d):
+    def rows_of(at):
+        return pl.ds(pl.multiple_of(at * 32, 32), 32)
+
+    def along_z(d):
         return pltpu.make_async_remote_copy(
-            src_ref=part.at[slice_of((occ + d) % 8), :],
+            src_ref=part.at[rows_of((z_at + d) % 4), :],
             dst_ref=gath.at[d - 1],
             send_sem=red_s.at[d],
             recv_sem=red_r.at[d],
-            device_id=occ_peer(d, 0),
+            device_id=near(d, 0, 0),
             device_id_type=MESH,
         )
 
-    for d in range(1, 8):
-        reduce_to(d).start()
+    for d in range(1, 4):
+        along_z(d).start()
+    total = part[rows_of(z_at), :]
+    for d in range(1, 4):
+        along_z(d).wait_recv()
+        total = total + gath[d - 1]
+    mine[...] = total
+    along_y = pltpu.make_async_remote_copy(
+        src_ref=mine,
+        dst_ref=gath.at[3],
+        send_sem=red_s.at[0],
+        recv_sem=red_r.at[0],
+        device_id=near(0, 1, 0),
+        device_id_type=MESH,
+    )
+    along_y.start()
     start_in(FIRST, SECOND)
-    total = part[slice_of(occ), :]
-    for d in range(1, 8):
-        reduce_to(d).wait_recv()
-        total = total + gath[d - 1]
-    mine[...] = total.astype(jnp.bfloat16)
-    place = pl.ds(pl.multiple_of(core * 128 + occ * 16, 16), 16)
-    full[place, :] = total.astype(jnp.bfloat16)
+    along_y.wait_recv()
+    place = pl.ds(pl.multiple_of(core * 128 + z_at * 32, 32), 32)
+    full[place, :] = (mine[...] + gath[3]).astype(jnp.bfloat16)
 
     def share(n):
         d, e = others[n]
         return pltpu.make_async_remote_copy(
-            src_ref=mine,
+            src_ref=full.at[place, :],
             dst_ref=full.at[place, :],
             send_sem=all_s.at[n],
             recv_sem=all_r.at[n],
-            device_id=occ_peer(d, e),
+            device_id=near(d, 0, e),
             device_id_type=MESH,
         )
 
@@ -226,8 +239,9 @@
             send_back(i, s).start()
         keep_back(s).start()
 
-    for d in range(1, 8):
-        reduce_to(d).wait_send()
+    for d in range(1, 4):
+        along_z(d).wait_send()
+    along_y.wait_send()
     for n in range(len(others)):
         share(n).wait_send()
 
@@ -248,14 +262,15 @@
     vectors = cholesky.shape[0]
     return pl.pallas_call(
         kernel,
-        out_shape=jax.ShapeDtypeStruct(amplitudes.shape, jnp.bfloat16),
+        out_shape=pltpu.VMEM(amplitudes.shape, jnp.bfloat16),
         in_specs=[
-            pl.BlockSpec(memory_space=pltpu.SMEM),
+            pl.BlockSpec(memory_space=pl.ANY),
             pl.BlockSpec(memory_space=pl.ANY),
             pl.BlockSpec(memory_space=pl.ANY),
         ],
         out_specs=pl.BlockSpec(memory_space=pl.ANY),
         scratch_shapes=[
+            pltpu.SMEM(virtual_order.shape, jnp.int32),
             pltpu.VMEM((16 * rows, width), jnp.bfloat16),
             pltpu.VMEM((16 * rows, width), jnp.bfloat16),
             pltpu.VMEM(cholesky.shape, jnp.bfloat16),
@@ -264,27 +279,28 @@
             pltpu.VMEM((128, vectors), jnp.bfloat16),
             pltpu.VMEM((8, 64, 128), jnp.float32),
             pltpu.VMEM((128, 1024), jnp.float32),
-            pltpu.VMEM((7, 16, 1024), jnp.float32),
-            pltpu.VMEM((16, 1024), jnp.bfloat16),
+            pltpu.VMEM((4, 32, 1024), jnp.float32),
+            pltpu.VMEM((32, 1024), jnp.float32),
             pltpu.VMEM((256, 1024), jnp.bfloat16),
             pltpu.VMEM((512, 512), jnp.bfloat16),
             sems((peers, CHUNKS)),
             sems((peers, CHUNKS)),
             sems((peers, CHUNKS)),
             sems((peers, CHUNKS)),
-            sems((8,)),
-            sems((8,)),
-            sems((15,)),
-            sems((15,)),
+            sems((4,)),
+            sems((4,)),
+            sems((7,)),
+            sems((7,)),
             sems,
             sems((CHUNKS,)),
             sems,
+            sems,
         ],
         compiler_params=pltpu.CompilerParams(
-            collective_id=0, has_side_effects=True, vmem_limit_bytes=64000 * 1024
+            collective_id=0, has_side_effects=True, vmem_limit_bytes=44000 * 1024
         ),
         name="ladder",
-    )(virtual_order, amplitudes, cholesky)
+    )(pltpu.with_memory_space_constraint(virtual_order, pltpu.HBM), amplitudes, pltpu.with_memory_space_constraint(cholesky, pltpu.HBM))
 
 
 def solution(mesh):

time: 266 us -> 246 us (0.925)
  Pallas kernels: 254 us -> 241 us
  local copies, waits for them, and re-layouts: 9.16 us -> 4.09 us
    pallas_call x1, Pallas kernels: 254 us -> 241 us  [body(): pl.pallas_call(kernel, out_shape=pltpu.VMEM(amplitudes.shape, jnp.bfloat1...]
    unnamed x1, local copies, waits for them, and re-layouts: 9.16 us -> 4.09 us
where the time goes in v2:
time: 246 us
  Pallas kernels  241 us (98%)
  local copies, waits for them, and re-layouts  4.09 us (2%)
    pallas_call x1, Pallas kernels, body(): pl.pallas_call(kernel, out_shape=pltpu.VMEM(amplitudes.shape, jnp.bfloat1...  241 us

profile of v2, /device:TPU:1, one launch (start us, length us, event | category | flops | bytes accessed | tf_op | source)
XLA Modules:
  0.0 245.6 jit_solution(4703643937447536747)
XLA Ops:
  0.0 241.5 %ladder.1 = bf16[8,32,20480]{2,1,0:T(8,128)(2,1)S(1)} custom-call(s32[64]{0:T(128)} %orbitals.1, bf16[8,32,20480]{2,1,0:T(8,128)(2,1)} %amp.1, bf16[512,4096]{1,0:T(8,128)(2,1)} %chol.1), custom_call_target="tpu_custom_call" | custom-call | tf_op jit(solution)/shard_map/ladder/pallas_call | solution.py:263
  241.5 4.1 %copy.5 = bf16[8,32,20480]{2,1,0:T(8,128)(2,1)} copy(bf16[8,32,20480]{2,1,0:T(8,128)(2,1)S(1)} %ladder.1) | data formatting | bytes 20971520

commit v3 on v2

--- a/solution.py
+++ b/solution.py
@@ -9,9 +9,12 @@
 
 MESH = pl.DeviceIdType.MESH
 CHUNKS = 8
-FIRST, SECOND = 4, 6
+EARLY, FIRST, SECOND = 2, 4, 6
 HOPS = ((0, 1), (0, 3), (1, 0), (0, 2), (1, 1), (1, 3), (1, 2), (0, 0))
 PEERS = tuple((dy, dx, dc) for dc in (0, 1) for dy, dx in HOPS if (dy, dx, dc) != (0, 0, 0))
+NEAR = [i for i, at in enumerate(PEERS) if at[:2] in ((0, 1), (0, 3), (1, 0), (0, 0))]
+MIDDLE = [i for i, at in enumerate(PEERS) if at[:2] in ((0, 2), (1, 1), (1, 3))]
+FAR = [i for i, at in enumerate(PEERS) if at[:2] == (1, 2)]
 NT = (((1,), (1,)), ((), ()))
 
 
@@ -31,6 +34,7 @@
     orbitals, amp, chol, res,
     order, slots, out, vec, srt, brow, arow, gram, part, gath, mine, full, ints,
     in_s, in_r, back_s, back_r, red_s, red_r, all_s, all_r, own_in, own_out, vec_sem, order_sem,
+    x_sem, z_sem, far_sem,
 ):
     blk, occ = lax.axis_index("blk"), lax.axis_index("occ")
     y_hi, x_at, core = blk // 8, blk // 2 % 4, blk % 2
@@ -59,13 +63,15 @@
     )
     keep.start()
 
+    def signal(sem, device):
+        pl.semaphore_signal(sem, inc=1, device_id=device, device_id_type=MESH)
+
     barrier = pltpu.get_barrier_semaphore()
-    for offset in PEERS:
-        pl.semaphore_signal(barrier, inc=1, device_id={"blk": peer(offset)}, device_id_type=MESH)
-    around = [(d, 0, e) for d, e in others if d] + [(0, 1, 0)]
-    for at in around:
-        pl.semaphore_signal(barrier, inc=1, device_id=near(*at), device_id_type=MESH)
-    pl.semaphore_wait(barrier, len(PEERS) + len(around))
+    for i in NEAR:
+        signal(barrier, {"blk": peer(PEERS[i])})
+    for d, f in ((1, 0), (3, 0), (0, 1)):
+        signal(barrier, near(d, f, 0))
+    pl.semaphore_wait(barrier, len(NEAR) + 3)
 
     def columns(half, s):
         return pl.ds(pl.multiple_of(half * width + s * step, 128), step)
@@ -100,13 +106,22 @@
             out.at[block(blk), columns(0, s)], res.at[sym, :, columns(core, s)], own_out.at[s]
         )
 
-    def start_in(first, last):
+    def start_in(first, last, which=range(len(PEERS))):
         @pl.loop(first, last)
         def _(s):
-            for i in range(len(PEERS)):
+            for i in which:
                 send_in(i, s).start()
 
-    start_in(0, FIRST)
+    start_in(0, EARLY, NEAR)
+    for dx in (1, 3):
+        signal(x_sem, {"blk": peer((0, dx, 0))})
+        signal(z_sem, near(dx, 0, 0))
+    pl.semaphore_wait(x_sem, 2)
+    start_in(0, EARLY, MIDDLE)
+    signal(far_sem, {"blk": peer((0, 3, 0))})
+    pl.semaphore_wait(far_sem, 1)
+    start_in(0, EARLY, FAR)
+    start_in(EARLY, FIRST)
 
     read.wait()
     target = iota((256, 1), 0)
@@ -170,6 +185,7 @@
             device_id_type=MESH,
         )
 
+    pl.semaphore_wait(z_sem, 2)
     for d in range(1, 4):
         along_z(d).start()
     total = part[rows_of(z_at), :]
@@ -295,6 +311,9 @@
             sems((CHUNKS,)),
             sems,
             sems,
+            pltpu.SemaphoreType.REGULAR,
+            pltpu.SemaphoreType.REGULAR,
+            pltpu.SemaphoreType.REGULAR,
         ],
         compiler_params=pltpu.CompilerParams(
             collective_id=0, has_side_effects=True, vmem_limit_bytes=44000 * 1024

time: 246 us -> 245 us (level)
  no operation moved by 1% of the time
where the time goes in v3:
time: 245 us
  Pallas kernels  241 us (98%)
  local copies, waits for them, and re-layouts  4.09 us (2%)
    pallas_call x1, Pallas kernels, body(): pl.pallas_call(kernel, out_shape=pltpu.VMEM(amplitudes.shape, jnp.bfloat1...  241 us

profile of v3, /device:TPU:1, one launch (start us, length us, event | category | flops | bytes accessed | tf_op | source)
XLA Modules:
  0.0 244.9 jit_solution(17240549227341382444)
XLA Ops:
  0.0 240.8 %ladder.1 = bf16[8,32,20480]{2,1,0:T(8,128)(2,1)S(1)} custom-call(s32[64]{0:T(128)} %orbitals.1, bf16[8,32,20480]{2,1,0:T(8,128)(2,1)} %amp.1, bf16[512,4096]{1,0:T(8,128)(2,1)} %chol.1), custom_call_target="tpu_custom_call" | custom-call | tf_op jit(solution)/shard_map/ladder/pallas_call | solution.py:279
  240.8 4.1 %copy.5 = bf16[8,32,20480]{2,1,0:T(8,128)(2,1)} copy(bf16[8,32,20480]{2,1,0:T(8,128)(2,1)S(1)} %ladder.1) | data formatting | bytes 20971520

commit v4 on v3

--- a/solution.py
+++ b/solution.py
@@ -69,9 +69,15 @@
     barrier = pltpu.get_barrier_semaphore()
     for i in NEAR:
         signal(barrier, {"blk": peer(PEERS[i])})
-    for d, f in ((1, 0), (3, 0), (0, 1)):
-        signal(barrier, near(d, f, 0))
-    pl.semaphore_wait(barrier, len(NEAR) + 3)
+
+    members = [(d, f) for d in range(4) for f in range(2) if (d, f) != (0, 0)]
+
+    @pl.when(occ == 0)
+    def _():
+        for d, f in members:
+            signal(barrier, near(d, f, 0))
+
+    pl.semaphore_wait(barrier, len(NEAR) + jnp.where(occ == 0, 0, 1))
 
     def columns(half, s):
         return pl.ds(pl.multiple_of(half * width + s * step, 128), step)
@@ -115,7 +121,11 @@
     start_in(0, EARLY, NEAR)
     for dx in (1, 3):
         signal(x_sem, {"blk": peer((0, dx, 0))})
-        signal(z_sem, near(dx, 0, 0))
+
+    @pl.when(occ != 0)
+    def _():
+        signal(z_sem, {"blk": blk, "occ": 0})
+
     pl.semaphore_wait(x_sem, 2)
     start_in(0, EARLY, MIDDLE)
     signal(far_sem, {"blk": peer((0, 3, 0))})
@@ -185,7 +195,16 @@
             device_id_type=MESH,
         )
 
-    pl.semaphore_wait(z_sem, 2)
+    @pl.when(occ == 0)
+    def _():
+        pl.semaphore_wait(z_sem, len(members))
+        for d, f in members:
+            signal(z_sem, near(d, f, 0))
+
+    @pl.when(occ != 0)
+    def _():
+        pl.semaphore_wait(z_sem, 1)
+
     for d in range(1, 4):
         along_z(d).start()
     total = part[rows_of(z_at), :]

time: 245 us -> 244 us (level)
  no operation moved by 1% of the time
where the time goes in v4:
time: 244 us
  Pallas kernels  240 us (98%)
  local copies, waits for them, and re-layouts  4.09 us (2%)
    pallas_call x1, Pallas kernels, body(): pl.pallas_call(kernel, out_shape=pltpu.VMEM(amplitudes.shape, jnp.bfloat1...  240 us

profile of v4, /device:TPU:1, one launch (start us, length us, event | category | flops | bytes accessed | tf_op | source)
XLA Modules:
  0.0 244.2 jit_solution(4404224356764764873)
XLA Ops:
  0.0 240.1 %ladder.1 = bf16[8,32,20480]{2,1,0:T(8,128)(2,1)S(1)} custom-call(s32[64]{0:T(128)} %orbitals.1, bf16[8,32,20480]{2,1,0:T(8,128)(2,1)} %amp.1, bf16[512,4096]{1,0:T(8,128)(2,1)} %chol.1), custom_call_target="tpu_custom_call" | custom-call | tf_op jit(solution)/shard_map/ladder/pallas_call | solution.py:298
  240.1 4.1 %copy.5 = bf16[8,32,20480]{2,1,0:T(8,128)(2,1)} copy(bf16[8,32,20480]{2,1,0:T(8,128)(2,1)S(1)} %ladder.1) | data formatting | bytes 20971520

commit v5 on v4

--- a/solution.py
+++ b/solution.py
@@ -11,7 +11,12 @@
 CHUNKS = 8
 EARLY, FIRST, SECOND = 2, 4, 6
 HOPS = ((0, 1), (0, 3), (1, 0), (0, 2), (1, 1), (1, 3), (1, 2), (0, 0))
-PEERS = tuple((dy, dx, dc) for dc in (0, 1) for dy, dx in HOPS if (dy, dx, dc) != (0, 0, 0))
+PEERS = tuple(
+    (dy, dx, (dc + i) % 2)
+    for dc in (0, 1)
+    for i, (dy, dx) in enumerate(HOPS)
+    if (dy, dx, (dc + i) % 2) != (0, 0, 0)
+)
 NEAR = [i for i, at in enumerate(PEERS) if at[:2] in ((0, 1), (0, 3), (1, 0), (0, 0))]
 MIDDLE = [i for i, at in enumerate(PEERS) if at[:2] in ((0, 2), (1, 1), (1, 3))]
 FAR = [i for i, at in enumerate(PEERS) if at[:2] == (1, 2)]
@@ -289,13 +294,21 @@
         keep_back(s).wait()
 
 
+def store(held, res, sem):
+    copies = [pltpu.make_async_copy(held.at[g], res.at[g], sem.at[g]) for g in range(held.shape[0])]
+    for copy in copies:
+        copy.start()
+    for copy in copies:
+        copy.wait()
+
+
 def body(amplitudes, cholesky, virtual_order):
     groups, rows, columns = amplitudes.shape
     width = columns // 2
     sems = pltpu.SemaphoreType.DMA
     peers = len(PEERS)
     vectors = cholesky.shape[0]
-    return pl.pallas_call(
+    result = pl.pallas_call(
         kernel,
         out_shape=pltpu.VMEM(amplitudes.shape, jnp.bfloat16),
         in_specs=[
@@ -339,6 +352,15 @@
         ),
         name="ladder",
     )(pltpu.with_memory_space_constraint(virtual_order, pltpu.HBM), amplitudes, pltpu.with_memory_space_constraint(cholesky, pltpu.HBM))
+    return pl.pallas_call(
+        store,
+        out_shape=jax.ShapeDtypeStruct(amplitudes.shape, jnp.bfloat16),
+        in_specs=[pl.BlockSpec(memory_space=pl.ANY)],
+        out_specs=pl.BlockSpec(memory_space=pl.ANY),
+        scratch_shapes=[sems((groups,))],
+        compiler_params=pltpu.CompilerParams(vmem_limit_bytes=1024 * 1024),
+        name="store",
+    )(result)
 
 
 def solution(mesh):

time: 244 us -> 244 us (level)
  local copies, waits for them, and re-layouts: 4.09 us -> 0 us
  Pallas kernels: 240 us -> 244 us
    unnamed x1 -> x0, local copies, waits for them, and re-layouts: 4.09 us -> none
    pallas_call x0 -> x1, Pallas kernels: none -> 4.04 us  [body(): pl.pallas_call(store, out_shape=jax.ShapeDtypeStruct(amplitudes.shape, jn...]
where the time goes in v5:
time: 244 us
  Pallas kernels  244 us (100%)
    pallas_call x1, Pallas kernels, body(): pl.pallas_call(kernel, out_shape=pltpu.VMEM(amplitudes.shape, jnp.bfloat1...  240 us

profile of v5, /device:TPU:1, one launch (start us, length us, event | category | flops | bytes accessed | tf_op | source)
XLA Modules:
  0.0 244.1 jit_solution(16843189624714704009)
XLA Ops:
  0.0 240.1 %ladder.1.held = bf16[8,32,20480]{2,1,0:T(8,128)(2,1)S(1)} custom-call(s32[64]{0:T(128)} %orbitals.1, bf16[8,32,20480]{2,1,0:T(8,128)(2,1)} %amp.1, bf16[512,4096]{1,0:T(8,128)(2,1)} %chol.1), custom_call_target="tpu_custom_call" | custom-call | tf_op jit(solution)/shard_map/ladder/pallas_call | solution.py:311
  240.1 4.0 %store.1 = bf16[8,32,20480]{2,1,0:T(8,128)(2,1)} custom-call(bf16[8,32,20480]{2,1,0:T(8,128)(2,1)S(1)} %ladder.1.held), custom_call_target="tpu_custom_call" | custom-call | tf_op jit(solution)/shard_map/store/pallas_call | solution.py:355
